TPU v7x, 256 devices: a whole 4x4x8 slice. The times are simulated.
256 devices in a mesh: seq: 32 (over x, z), head: 8 (over y, core).
Axes of the slice: x: 4, y: 4, z: 8, core: 2. Of those that a mesh axis runs over, the one named last changes fastest.
Arguments:
- tokens: bfloat16 [24576, 4096], P('seq'), may hold values from -6 to 6
- qkv_weight: bfloat16 [3, 4096, 4096], P(None, 'seq', 'head'), may hold values from -0.09375 to 0.09375
- out_weight: bfloat16 [4096, 4096], P('head', 'seq'), may hold values from -0.09375 to 0.09375
- out_gain: float32 [4096], P('head'), may hold values from 0.25 to 1.75
Outputs:
- mixed: bfloat16 [24576, 4096], P('seq', 'head')
All inputs are finite; a program needn't handle non-finite values.
Results may differ from a plain program's by a relative error of at most 0.019.
Values may be sent and summed in bfloat16 or wider, within the bound.
No kernel may reach another device: no remote copies, remote signals or barrier semaphores. Data moves between devices by JAX's collectives and lax.ppermute only.
A program may use at most 64 MiB of HBM per device.

v0:
```python
import jax
import jax.numpy as jnp
from jax import lax
from jax.sharding import PartitionSpec as P

HEAD_DIM = 128


def carried_in(array, axis, join, neutral):
    place = lax.axis_index(axis)
    gathered = lax.all_gather(array.astype(jnp.bfloat16), axis)
    state = jnp.zeros_like(array) + jnp.asarray(neutral, array.dtype)

    def one(step, state):
        return join(state, lax.dynamic_index_in_dim(gathered, step, 0, False).astype(array.dtype))

    return lax.fori_loop(0, place, one, state)


def per_device(tokens, qkv_weight, out_weight, out_gain):
    tok_rows = tokens.shape[0]
    width_dev = qkv_weight.shape[2]
    heads_dev = width_dev // HEAD_DIM

    def add_single(shard_piece):
        return jnp.dot(tokens, shard_piece, preferred_element_type=jnp.float32)

    query_part = add_single(lax.all_gather(qkv_weight[0], "seq", axis=0, tiled=True))
    key_part = add_single(lax.all_gather(qkv_weight[1], "seq", axis=0, tiled=True))
    value_part = add_single(lax.all_gather(qkv_weight[2], "seq", axis=0, tiled=True))
    projected = jnp.stack([query_part, key_part, value_part])
    projected = projected.astype(jnp.bfloat16).reshape(3, tok_rows, heads_dev, HEAD_DIM)
    query_matrix, local_key_rows, local_value_rows = (projected[0], projected[1], projected[2])
    local_state = jnp.einsum(
        "sbq,sbn->bqn", local_key_rows, local_value_rows, preferred_element_type=jnp.float32
    )
    zero_state = jnp.zeros_like(local_state)
    prefix_state_sum = carried_in(
        local_state, "seq", lambda earlier, later: earlier + later, zero_state
    )
    causal = jnp.tril(jnp.ones((tok_rows, tok_rows), dtype=bool))
    scores = jnp.einsum(
        "thk,shk->hts", query_matrix, local_key_rows, preferred_element_type=jnp.float32
    )
    scores = jnp.where(causal[None], scores, 0.0).astype(jnp.bfloat16)
    local_term = jnp.einsum(
        "hts,shv->thv", scores, local_value_rows, preferred_element_type=jnp.float32
    )
    carried_state = jnp.einsum(
        "mal,alr->mar",
        query_matrix,
        prefix_state_sum.astype(jnp.bfloat16),
        preferred_element_type=jnp.float32,
    )
    attended = local_term + carried_state
    inv_scale = lax.rsqrt(jnp.mean(attended * attended, axis=-1, keepdims=True) + 1e-06)
    normed = ((attended * inv_scale).reshape(tok_rows, width_dev) * out_gain).astype(jnp.bfloat16)
    partial_out = jnp.dot(
        normed,
        lax.all_gather(out_weight, "seq", axis=1, tiled=True),
        preferred_element_type=jnp.float32,
    )
    return lax.psum_scatter(
        partial_out.astype(jnp.bfloat16), "head", scatter_dimension=1, tiled=True
    )


def solution(mesh):
    return jax.shard_map(
        per_device,
        mesh=mesh,
        in_specs=(P("seq", None), P(None, "seq", "head"), P("head", "seq"), P("head")),
        out_specs=P("seq", "head"),
        check_vma=False,
    )
```

profile of v0, /device:TPU:1, one launch (start us, length us, event | category | flops | bytes accessed | tf_op | source)
XLA Modules:
  0.0 480.2 jit_solution(4706658048716186455)
XLA Ops:
  6.5 1.8 fusion.24
  8.3 0.0 all-gather.16.cloned.1.call-start
  8.4 0.7 all-gather.16.cloned.1.call-update
  9.1 0.7 all-gather.14.cloned.1.call-update
  9.9 82.1 %all-gather.12.cloned.1.call-done = bf16[1,4096,512]{2,1,0:T(8,128)(2,1)} async-done(((bf16[1,128,512]{2,1,0:T(8,128)(2,1)}), bf16[1,4096,512]{2,1,0:T(8,128)(2,1)}) %all-gather.12.cloned.1.call-update) | async-done | bytes 4194320 | tf_op jit(solution)/shard_map/all_gather | solution.py:30
  91.9 7.5 %fusion.13 = bf16[768,512]{0,1:T(8,128)(2,1)S(1)} fusion(bf16[768,4096]{1,0:T(8,128)(2,1)} %param.6, bf16[1,4096,512]{2,1,0:T(8,128)(2,1)} %all-gather.12.cloned.1.call-done), kind=kOutput, calls=%fused_computation.20 | convolution fusion | flops 3221618688 | bytes 11272192 | tf_op jit(solution)/shard_map/dot_general | solution.py:26
  99.4 73.6 %all-gather.16.cloned.1.call-done = bf16[1,4096,512]{2,1,0:T(8,128)(2,1)} async-done(((bf16[1,128,512]{2,1,0:T(8,128)(2,1)}), bf16[1,4096,512]{2,1,0:T(8,128)(2,1)}) %all-gather.16.cloned.1.call-update) | async-done | bytes 4194320 | tf_op jit(solution)/shard_map/all_gather | solution.py:29
  173.0 7.5 %fusion.19 = bf16[768,512]{0,1:T(8,128)(2,1)S(1)} fusion(bf16[768,4096]{1,0:T(8,128)(2,1)} %param.6, bf16[1,4096,512]{2,1,0:T(8,128)(2,1)} %all-gather.16.cloned.1.call-done), kind=kOutput, calls=%fused_computation.22 | convolution fusion | flops 3221618688 | bytes 11272192 | tf_op jit(solution)/shard_map/dot_general | solution.py:26
  180.5 0.9 copy-done
  181.4 1.0 convolution_convert_fusion.1
  182.5 0.5 all-gather.10.cloned.1.call-update
  183.0 0.2 reduce-scatter.2.cloned.1.call-start
  183.3 1.0 iota_compare_fusion
  184.3 69.9 %all-gather.14.cloned.1.call-done = bf16[1,4096,512]{2,1,0:T(8,128)(2,1)} async-done(((bf16[1,128,512]{2,1,0:T(8,128)(2,1)}), bf16[1,4096,512]{2,1,0:T(8,128)(2,1)}) %all-gather.14.cloned.1.call-update) | async-done | bytes 4194320 | tf_op jit(solution)/shard_map/all_gather | solution.py:28
  254.2 7.5 %fusion.16 = bf16[768,512]{0,1:T(8,128)(2,1)S(1)} fusion(bf16[768,4096]{1,0:T(8,128)(2,1)} %param.6, bf16[1,4096,512]{2,1,0:T(8,128)(2,1)} %all-gather.14.cloned.1.call-done), kind=kOutput, calls=%fused_computation.21 | convolution fusion | flops 3221618688 | bytes 11272192 | tf_op jit(solution)/shard_map/dot_general | solution.py:26
  261.6 4.2 fusion
  265.9 69.3 %all-gather.18.cloned.1.call-done = bf16[128,128,128]{2,1,0:T(8,128)(2,1)} async-done(((bf16[4,128,128]{2,1,0:T(8,128)(2,1)}), bf16[128,128,128]{2,1,0:T(8,128)(2,1)}) %all-gather.18.cloned.1.call-update) | async-done | bytes 4194320 | tf_op jit(solution)/shard_map/all_gather | solution.py:11
  335.2 0.4 fusion.12
  335.6 0.1 bitcast_multiply_fusion.1
  335.8 0.1 copy-done.1
  335.9 0.1 fusion.11
  336.0 81.7 %all-gather.10.cloned.1.call-done = bf16[512,4096]{1,0:T(8,128)(2,1)} async-done(((bf16[512,128]{1,0:T(8,128)(2,1)}), bf16[512,4096]{1,0:T(8,128)(2,1)}) %all-gather.10.cloned.1.call-update) | async-done | bytes 4194320 | tf_op jit(solution)/shard_map/all_gather | solution.py:60
  417.7 7.6 %convolution_convert_fusion = bf16[768,4096]{1,0:T(8,128)(2,1)} fusion(bf16[768,512]{0,1:T(8,128)(2,1)S(1)} %fusion.11, bf16[512,4096]{1,0:T(8,128)(2,1)} %all-gather.10.cloned.1.call-done), kind=kOutput, calls=%fused_computation.2 | convolution fusion | flops 3224371200 | bytes 11272192 | tf_op jit(solution)/shard_map/dot_general | solution.py:58
  425.2 48.1 %reduce-scatter.2.cloned.1.call-done = bf16[768,512]{1,0:T(8,128)(2,1)} async-done(((bf16[768,4096]{1,0:T(8,128)(2,1)}), bf16[768,512]{1,0:T(8,128)(2,1)}) %reduce-scatter.2.cloned.1.call-update) | async-done | bytes 786448 | tf_op jit(solution)/shard_map/reduce_scatter | solution.py:63
  (12 shorter events, 0.2 us)
Async XLA Ops:
  6.5 85.4 %all-gather.12.cloned.1.call-start = ((), (), s32[]{:S(2)}) async-start(), calls=%async_computation.3 | async-start | bytes 4325376 | tf_op jit(solution)/shard_map/all_gather | solution.py:30
  8.3 164.7 %all-gather.16.cloned.1.call-start = ((), (), s32[]{:S(2)}) async-start(), calls=%async_computation.5 | async-start | bytes 4325376 | tf_op jit(solution)/shard_map/all_gather | solution.py:29
  9.1 245.1 %all-gather.14.cloned.1.call-start = ((), (), s32[]{:S(2)}) async-start(), calls=%async_computation.4 | async-start | bytes 4325376 | tf_op jit(solution)/shard_map/all_gather | solution.py:28
  9.8 325.3 %all-gather.18.cloned.1.call-start = ((), (), s32[]{:S(2)}) async-start(), calls=%async_computation.6 | async-start | bytes 4325376 | tf_op jit(solution)/shard_map/all_gather | solution.py:11
  180.5 0.9 copy-start
  182.4 235.2 %all-gather.10.cloned.1.call-start = ((), (), s32[]{:S(2)}) async-start(), calls=%async_computation.1 | async-start | bytes 4325376 | tf_op jit(solution)/shard_map/all_gather | solution.py:60
  183.0 290.3 %reduce-scatter.2.cloned.1.call-start = ((), (), s32[]{:S(2)}) async-start(), calls=%async_computation.2 | async-start | bytes 7077888 | tf_op jit(solution)/shard_map/reduce_scatter | solution.py:63
  335.2 0.7 copy-start.1
Sparse Core Ops, SparseCore 0:
  9.9 81.9 all-gather.11
  94.5 78.4 all-gather.15
  175.6 78.4 all-gather.13
  256.6 78.4 all-gather.17
  337.4 80.1 all-gather.9
  425.4 47.8 reduce-scatter.1
where the time goes:
time: 481 us; the launch traced here: 480 us
  waiting for transfers between devices  427 us (89%)
  matrix products  35.6 us (7%)
  between operations  13.6 us (3%)
    all_gather x1, waiting for transfers between devices, per_device(): lax.all_gather(qkv_weight[2], 'seq', axis=0, tiled=True)  82.1 us
    all_gather x1, waiting for transfers between devices, per_device(): lax.all_gather(out_weight, 'seq', axis=1, tiled=True)  81.7 us
    all_gather x1, waiting for transfers between devices, per_device(): lax.all_gather(qkv_weight[1], 'seq', axis=0, tiled=True)  73.6 us
    all_gather x1, waiting for transfers between devices, per_device(): lax.all_gather(qkv_weight[0], 'seq', axis=0, tiled=True)  69.9 us
    all_gather x1, waiting for transfers between devices, carried_in(): gathered = lax.all_gather(array.astype(jnp.bfloat16), axis)  69.3 us
    reduce_scatter x1, waiting for transfers between devices, per_device(): lax.psum_scatter(partial_out.astype(jnp.bfloat16), 'head', scatter_dimens...  48.1 us
    dot_general x3, matrix products, add_single(): return jnp.dot(tokens, shard_piece, preferred_element_type=jnp.float32)  22.4 us
  transfers between devices with their start and end apart: 6, of which 6 were waited for; matrix products, arithmetic and copies ran while one was open for 6% of the time, Pallas kernels for 0%

commit v1 on v0

--- a/solution.py
+++ b/solution.py
@@ -1,9 +1,20 @@
+import functools
 import jax
 import jax.numpy as jnp
 from jax import lax
 from jax.sharding import PartitionSpec as P
 
 HEAD_DIM = 128
+
+
+def slabs_direct(inputs, join_dim, named_axis):
+    ready = lax.axis_size(named_axis)
+    inter = jnp.stack([inputs] * ready)
+    tall = lax.all_to_all(inter, axis_name=named_axis, split_axis=0, concat_axis=0)
+    return jnp.concatenate(tall, axis=join_dim)
+
+
+trails_divide = functools.partial(slabs_direct, join_dim=0, named_axis="seq")
 
 
 def carried_in(array, axis, join, neutral):
@@ -27,7 +38,7 @@
 
     query_part = add_single(lax.all_gather(qkv_weight[0], "seq", axis=0, tiled=True))
     key_part = add_single(lax.all_gather(qkv_weight[1], "seq", axis=0, tiled=True))
-    value_part = add_single(lax.all_gather(qkv_weight[2], "seq", axis=0, tiled=True))
+    value_part = add_single(trails_divide(qkv_weight[2]))
     projected = jnp.stack([query_part, key_part, value_part])
     projected = projected.astype(jnp.bfloat16).reshape(3, tok_rows, heads_dev, HEAD_DIM)
     query_matrix, local_key_rows, local_value_rows = (projected[0], projected[1], projected[2])

time: 481 us -> 448 us (0.931)
  waiting for transfers between devices: 427 us -> 379 us
  starting transfers between devices: 0.38 us -> 12.3 us
    all_to_all x0 -> x1, waiting for transfers between devices: none -> 111 us  [slabs_direct(): lax.all_to_all(inter, axis_name=named_axis, split_axis=0, concat_axis=0)]
    all_gather x1 -> x0, waiting for transfers between devices: 82.1 us -> none  [per_device(): lax.all_gather(qkv_weight[2], 'seq', axis=0, tiled=True)]
    all_gather x1, waiting for transfers between devices: 73.6 us -> 0.02 us  [per_device(): lax.all_gather(qkv_weight[1], 'seq', axis=0, tiled=True)]
    all_to_all x0 -> x1, starting transfers between devices: none -> 12 us  [slabs_direct(): lax.all_to_all(inter, axis_name=named_axis, split_axis=0, concat_axis=0)]
  transfers between devices with their start and end apart: 6 -> 6, of which waited for: 6 -> 5; matrix products, arithmetic and copies ran while one was open for 6% -> 7% of each run, Pallas kernels for 0% -> 0%
where the time goes in v1:
time: 448 us; the launch traced here: 447 us
  waiting for transfers between devices  379 us (85%)
  matrix products  35.7 us (8%)
  between operations  13.2 us (3%)
  starting transfers between devices  12.3 us (3%)
  local copies, waits for them, and re-layouts  5.16 us (1%)
    all_to_all x1, waiting for transfers between devices, slabs_direct(): lax.all_to_all(inter, axis_name=named_axis, split_axis=0, concat_axis=0)  111 us
    all_gather x1, waiting for transfers between devices, per_device(): lax.all_gather(out_weight, 'seq', axis=1, tiled=True)  81.7 us
    all_gather x1, waiting for transfers between devices, carried_in(): gathered = lax.all_gather(array.astype(jnp.bfloat16), axis)  69.4 us
    all_gather x1, waiting for transfers between devices, per_device(): lax.all_gather(qkv_weight[0], 'seq', axis=0, tiled=True)  67.7 us
    reduce_scatter x1, waiting for transfers between devices, per_device(): lax.psum_scatter(partial_out.astype(jnp.bfloat16), 'head', scatter_dimens...  48 us
    dot_general x3, matrix products, add_single(): return jnp.dot(tokens, shard_piece, preferred_element_type=jnp.float32)  22.4 us
    all_to_all x1, starting transfers between devices, slabs_direct(): lax.all_to_all(inter, axis_name=named_axis, split_axis=0, concat_axis=0)  12 us
  transfers between devices with their start and end apart: 6, of which 5 were waited for; matrix products, arithmetic and copies ran while one was open for 7% of the time, Pallas kernels for 0%

profile of v1, /device:TPU:1, one launch (start us, length us, event | category | flops | bytes accessed | tf_op | source)
XLA Modules:
  0.0 447.0 jit_solution(575144732228990517)
XLA Ops:
  6.5 1.8 fusion.19
  8.3 2.4 stack.11
  10.7 12.0 %all-to-all-start = ((bf16[32,128,512]{2,1,0:T(8,128)(2,1)}), bf16[32,128,512]{2,1,0:T(8,128)(2,1)}, u32[]{:S(2)}, u32[]{:S(2)}) async-start(bf16[32,128,512]{2,1,0:T(8,128)(2,1)} %stack.11), calls=%async_computation | async-start | bytes 8388608 | tf_op jit(solution)/shard_map/all_to_all | solution.py:13
  22.7 0.0 all-gather.10.cloned.1.call-start
  22.8 0.7 all-gather.10.cloned.1.call-update
  23.5 111.1 %all-to-all-done = bf16[32,128,512]{2,1,0:T(8,128)(2,1)} async-done(((bf16[32,128,512]{2,1,0:T(8,128)(2,1)}), bf16[32,128,512]{2,1,0:T(8,128)(2,1)}, u32[]{:S(2)}, u32[]{:S(2)}) %all-to-all-start) | async-done | bytes 4194336 | tf_op jit(solution)/shard_map/all_to_all | solution.py:13
  134.7 7.5 %convolution_convert_fusion.1 = bf16[768,512]{0,1:T(8,128)(2,1)S(1)} fusion(bf16[768,4096]{1,0:T(8,128)(2,1)} %param.6, bf16[4096,512]{1,0:T(8,128)(2,1)} %bitcast.2), kind=kOutput, calls=%fused_computation.20 | convolution fusion | flops 3221618688 | bytes 11272192 | tf_op jit(solution)/shard_map/dot_general | solution.py:37
  142.2 7.5 %fusion.14 = bf16[768,512]{0,1:T(8,128)(2,1)S(1)} fusion(bf16[768,4096]{1,0:T(8,128)(2,1)} %param.6, bf16[1,4096,512]{2,1,0:T(8,128)(2,1)} %all-gather.12.cloned.1.call-done), kind=kOutput, calls=%fused_computation.19 | convolution fusion | flops 3221618688 | bytes 11272192 | tf_op jit(solution)/shard_map/dot_general | solution.py:37
  149.7 0.9 copy-done
  150.5 1.0 convolution_convert_fusion.2
  151.7 0.5 all-gather.8.cloned.1.call-update
  152.2 0.2 reduce-scatter.2.cloned.1.call-start
  152.4 1.0 iota_compare_fusion
  153.4 67.7 %all-gather.10.cloned.1.call-done = bf16[1,4096,512]{2,1,0:T(8,128)(2,1)} async-done(((bf16[1,128,512]{2,1,0:T(8,128)(2,1)}), bf16[1,4096,512]{2,1,0:T(8,128)(2,1)}) %all-gather.10.cloned.1.call-update) | async-done | bytes 4194320 | tf_op jit(solution)/shard_map/all_gather | solution.py:39
  221.1 7.5 %fusion.11 = bf16[768,512]{0,1:T(8,128)(2,1)S(1)} fusion(bf16[768,4096]{1,0:T(8,128)(2,1)} %param.6, bf16[1,4096,512]{2,1,0:T(8,128)(2,1)} %all-gather.10.cloned.1.call-done), kind=kOutput, calls=%fused_computation.18 | convolution fusion | flops 3221618688 | bytes 11272192 | tf_op jit(solution)/shard_map/dot_general | solution.py:37
  228.6 4.2 fusion
  232.8 69.4 %all-gather.14.cloned.1.call-done = bf16[128,128,128]{2,1,0:T(8,128)(2,1)} async-done(((bf16[4,128,128]{2,1,0:T(8,128)(2,1)}), bf16[128,128,128]{2,1,0:T(8,128)(2,1)}) %all-gather.14.cloned.1.call-update) | async-done | bytes 4194320 | tf_op jit(solution)/shard_map/all_gather | solution.py:22
  302.3 0.4 fusion.10
  302.8 0.1 bitcast_multiply_fusion.1
  302.9 0.1 copy-done.1
  303.0 0.1 fusion.9
  303.1 81.7 %all-gather.8.cloned.1.call-done = bf16[512,4096]{1,0:T(8,128)(2,1)} async-done(((bf16[512,128]{1,0:T(8,128)(2,1)}), bf16[512,4096]{1,0:T(8,128)(2,1)}) %all-gather.8.cloned.1.call-update) | async-done | bytes 4194320 | tf_op jit(solution)/shard_map/all_gather | solution.py:71
  384.8 7.6 %convolution_convert_fusion = bf16[768,4096]{1,0:T(8,128)(2,1)} fusion(bf16[768,512]{0,1:T(8,128)(2,1)S(1)} %fusion.9, bf16[512,4096]{1,0:T(8,128)(2,1)} %all-gather.8.cloned.1.call-done), kind=kOutput, calls=%fused_computation.2 | convolution fusion | flops 3224371200 | bytes 11272192 | tf_op jit(solution)/shard_map/dot_general | solution.py:69
  392.4 48.0 %reduce-scatter.2.cloned.1.call-done = bf16[768,512]{1,0:T(8,128)(2,1)} async-done(((bf16[768,4096]{1,0:T(8,128)(2,1)}), bf16[768,512]{1,0:T(8,128)(2,1)}) %reduce-scatter.2.cloned.1.call-update) | async-done | bytes 786448 | tf_op jit(solution)/shard_map/reduce_scatter | solution.py:74
  (12 shorter events, 0.2 us)
Async XLA Ops:
  6.5 135.6 %all-gather.12.cloned.1.call-start = ((), (), s32[]{:S(2)}) async-start(), calls=%async_computation.5 | async-start | bytes 4325376 | tf_op jit(solution)/shard_map/all_gather | solution.py:40
  10.7 123.9 %all-to-all-start = ((bf16[32,128,512]{2,1,0:T(8,128)(2,1)}), bf16[32,128,512]{2,1,0:T(8,128)(2,1)}, u32[]{:S(2)}, u32[]{:S(2)}) async-start(bf16[32,128,512]{2,1,0:T(8,128)(2,1)} %stack.11), calls=%async_computation | async-start | bytes 8388608 | tf_op jit(solution)/shard_map/all_to_all | solution.py:13
  22.7 198.4 %all-gather.10.cloned.1.call-start = ((), (), s32[]{:S(2)}) async-start(), calls=%async_computation.4 | async-start | bytes 4325376 | tf_op jit(solution)/shard_map/all_gather | solution.py:39
  23.5 278.8 %all-gather.14.cloned.1.call-start = ((), (), s32[]{:S(2)}) async-start(), calls=%async_computation.6 | async-start | bytes 4325376 | tf_op jit(solution)/shard_map/all_gather | solution.py:22
  149.7 0.9 copy-start
  151.6 233.2 %all-gather.8.cloned.1.call-start = ((), (), s32[]{:S(2)}) async-start(), calls=%async_computation.2 | async-start | bytes 4325376 | tf_op jit(solution)/shard_map/all_gather | solution.py:71
  152.2 288.2 %reduce-scatter.2.cloned.1.call-start = ((), (), s32[]{:S(2)}) async-start(), calls=%async_computation.3 | async-start | bytes 7077888 | tf_op jit(solution)/shard_map/reduce_scatter | solution.py:74
  302.3 0.7 copy-start.1
Sparse Core Ops, SparseCore 0:
  9.9 131.5 all-gather.11
  144.1 76.9 all-gather.9
  223.7 78.4 all-gather.13
  304.6 80.1 all-gather.7
  392.5 47.8 reduce-scatter.1
